TPU v7x, 256 devices: a whole 4x4x8 slice. The times are simulated.
256 devices in a mesh: node: 16 (over z, core), trow: 4 (over x), tcol: 4 (over y).
Axes of the slice: x: 4, y: 4, z: 8, core: 2. Of those that a mesh axis runs over, the one named last changes fastest.
Arguments:
- near_blocks: bfloat16 [1024, 8, 256, 256], P(('node', 'trow'), 'tcol'), may hold values from -27 to 75, as said below
- leaf_bases: bfloat16 [1024, 256, 256], P(('node', 'trow')), may hold values from -1 to 1, as said below
- upper_bases: bfloat16 [512, 256, 256], P(('node', 'trow', 'tcol')), may hold values from -1 to 1, as said below
- neighbours: int32 [1024, 8], P(('node', 'trow'), 'tcol'), may hold values from 0 to 1023, as said below
Outputs:
- skeleton: float32 [1024, 8, 128, 128], P(('node', 'trow'), 'tcol')
- upper_skeleton: float32 [512, 5, 128, 128], P(('node', 'trow', 'tcol'))
Inputs may be any that keep to these rules, and one draw needn't show every extreme that they name: `neighbours`: slot 0 of row i is i, slot 1 is its sibling i XOR 1, and slots 2 to 7 are six distinct leaves among 2 (i // 2) - 4, -3, -2, -1, +2, +3, +4, +5, taken modulo 1024. near_blocks[i, 0] is symmetric and positive definite. `leaf_bases`: each leaf basis is an orthogonal matrix rounded to bfloat16. `upper_bases`: each node basis is an orthogonal matrix rounded to bfloat16.
All inputs are finite; a program needn't handle non-finite values.
Results may differ from a plain program's by a relative error of at most 0.0038.
Values may be sent and summed in bfloat16 or wider, within the bound.
A program may use at most 64 MiB of HBM per device.

v0:
```python
import jax
import jax.numpy as jnp
from jax import lax
from jax.sharding import PartitionSpec as P

BLK = 256
RANK = 128


def with_halo(array, sides, width):
    for axis, dim in sides:
        count, length = (lax.axis_size(axis), array.shape[dim])
        up = [(i, (i + 1) % count) for i in range(count)]
        down = [(j, i) for i, j in up]
        last = lax.slice_in_dim(array, length - width, length, axis=dim)
        initial = lax.slice_in_dim(array, 0, width, axis=dim)
        before = lax.ppermute(last, axis, up)
        after = lax.ppermute(initial, axis, down)
        array = jnp.concatenate([before, array, after], axis=dim)
    return array


def filled_up(lines, count):
    spare = -lines.shape[0] % count
    if not spare:
        return lines
    return jnp.concatenate([lines, jnp.zeros((spare, *lines.shape[1:]), lines.dtype)])


def spread(array, axis, root):
    lines = jnp.where(lax.axis_index(axis) == root, array, jnp.zeros_like(array)).reshape(
        -1, *array.shape[1:][-1:]
    )
    padded = filled_up(lines, lax.axis_size(axis))
    own = lax.psum_scatter(padded, axis, scatter_dimension=0, tiled=True)
    return lax.all_gather(own, axis, axis=0, tiled=True)[: len(lines)].reshape(array.shape)


def eliminate(rotated, spare_size):
    corner = rotated[..., :spare_size, :spare_size]
    factor = jnp.linalg.cholesky(0.5 * (corner + jnp.swapaxes(corner, -1, -2)))
    coupled = lax.linalg.triangular_solve(
        factor, rotated[..., :spare_size, spare_size:], left_side=True, lower=True
    )
    return (factor, coupled)


def reduce_rows(rotated, factor, coupled, spare_size):
    widened = jnp.broadcast_to(factor[:, None], rotated.shape[:2] + factor.shape[1:])
    solved = lax.linalg.triangular_solve(
        widened, rotated[..., :spare_size, spare_size:], left_side=True, lower=True
    )
    return rotated[..., spare_size:, spare_size:] - jnp.einsum(
        "lxr,lkxs->lkrs", coupled, solved, precision=lax.Precision.HIGHEST
    )


def arrange(blocks, parent_count, rank_size):
    shaped = blocks.reshape(parent_count, 2, 5, 2, rank_size, rank_size)
    return shaped.transpose(0, 2, 1, 4, 3, 5).reshape(parent_count, 5, 2 * rank_size, 2 * rank_size)


def per_device(near_blocks, leaf_bases, upper_bases, neighbours):
    leaf_count = near_blocks.shape[0]
    spare_size = BLK - RANK
    leaf_total = leaf_count * lax.axis_size(("node", "trow"))
    parents_all = leaf_total // 2
    first_leaf = lax.axis_index(("node", "trow")) * leaf_count
    widened = with_halo(leaf_bases, ((("node", "trow"), 0),), 5)
    position = (neighbours - first_leaf + leaf_total // 2) % leaf_total - leaf_total // 2 + 5
    partner = widened[position]
    turned = jnp.einsum(
        "lkab,lkbc->lkac", near_blocks, partner, preferred_element_type=jnp.float32
    ).astype(jnp.bfloat16)
    rotated = jnp.einsum("lba,lkbc->lkac", leaf_bases, turned, preferred_element_type=jnp.float32)
    factor, coupled = eliminate(rotated[:, 0], spare_size)
    shared = spread(jnp.concatenate([factor, coupled], axis=2), "tcol", 0)
    skeleton = reduce_rows(
        rotated, shared[:, :, :spare_size], shared[:, :, spare_size:], spare_size
    )
    packed = skeleton.astype(jnp.bfloat16)
    leaf_ids = first_leaf + jnp.arange(leaf_count, dtype=jnp.int32)
    target = 2 * ((neighbours // 2 - leaf_ids[:, None] // 2 + 2) % parents_all) + neighbours % 2
    labels = jnp.arange(10, dtype=jnp.int32)
    arrived, arrived_target = (
        lax.all_to_all(packed, "tcol", split_axis=0, concat_axis=1, tiled=True),
        lax.all_to_all(
            target.astype(jnp.bfloat16), "tcol", split_axis=0, concat_axis=1, tiled=True
        ),
    )
    selector = (arrived_target[:, :, None] == labels.astype(jnp.bfloat16)).astype(jnp.bfloat16)
    blocks = jnp.einsum("lkc,lkxy->lcxy", selector, arrived, preferred_element_type=jnp.float32)
    merged = arrange(blocks, arrived.shape[0] // 2, RANK).astype(jnp.bfloat16)
    parent_count = upper_bases.shape[0]
    extended = with_halo(upper_bases, ((("node", "trow", "tcol"), 0),), 2)
    partners = jnp.stack([extended[offset : offset + parent_count] for offset in range(5)], axis=1)
    upper_mixed = jnp.einsum(
        "pdab,pdbc->pdac", merged, partners, preferred_element_type=jnp.float32
    ).astype(jnp.bfloat16)
    lifted = jnp.einsum(
        "pba,pdbc->pdac", upper_bases, upper_mixed, preferred_element_type=jnp.float32
    )
    upper_factor, upper_coupled = eliminate(lifted[:, 2], RANK)
    upper_skeleton = reduce_rows(lifted, upper_factor, upper_coupled, RANK)
    return (skeleton, upper_skeleton)


def solution(mesh):
    return jax.shard_map(
        per_device,
        mesh=mesh,
        in_specs=(
            P(("node", "trow"), "tcol", None, None),
            P(("node", "trow"), None, None),
            P(("node", "trow", "tcol"), None, None),
            P(("node", "trow"), "tcol"),
        ),
        out_specs=(
            P(("node", "trow"), "tcol", None, None),
            P(("node", "trow", "tcol"), None, None, None),
        ),
        check_vma=False,
    )
```

profile of v0, /device:TPU:96, one launch (start us, length us, event | category | flops | bytes accessed | tf_op | source)
XLA Modules:
  0.0 975.4 jit_solution(10484452922178629279)
XLA Ops:
  8.6 1.6 collective-permute-start
  10.2 2.4 collective-permute-start.1
  12.8 11.3 %collective-permute-done = bf16[5,256,256]{2,1,0:T(8,128)(2,1)S(1)} collective-permute-done((bf16[5,256,256]{2,1,0:T(8,128)(2,1)S(1)}, bf16[5,256,256]{2,1,0:T(8,128)(2,1)S(1)}, u32[]{:S(2)}, u32[]{:S(2)}) %collective-permute-start) | collective-permute-done | bytes 655392 | tf_op jit(solution)/shard_map/ppermute | solution.py:17
  25.0 1.5 collective-permute-done.1
  26.5 2.1 pad_maximum_fusion
  28.6 2.8 gather_fusion
  31.4 4.9 convert_bitcast_fusion
  38.0 2.7 copy-done
  40.8 2.0 copy-done.2
  43.2 1.4 fusion.15
  45.0 187.5 %custom-call.20 = f32[16,128,128]{2,1,0:T(8,128)S(1)} custom-call(f32[16,128,128]{2,1,0:T(8,128)S(1)} %fusion.14), custom_call_target="Cholesky" | custom-call | tf_op jit(solution)/shard_map/jit(cholesky)/cholesky | solution.py:41
  233.0 157.6 %custom-call.21 = f32[16,1,128,128]{2,3,1,0:T(8,128)S(1)} custom-call(f32[16,1,128,128]{3,2,1,0:T(8,128)S(1)} %get-tuple-element.12), custom_call_target="InvertDiagBlocksLowerTriangular" | custom-call | tf_op jit(solution)/shard_map/triangular_solve | solution.py:42
  390.6 3.1 fusion.11
  393.7 1.5 maximum_select_fusion
  395.3 34.6 %reduce-scatter.2.cloned.1.call-done = f32[512,256]{1,0:T(8,128)} async-done(((f32[2048,256]{1,0:T(8,128)}), f32[512,256]{1,0:T(8,128)}) %reduce-scatter.2.cloned.1.call-update) | async-done | bytes 524304 | tf_op jit(solution)/shard_map/reduce_scatter | solution.py:35
  430.3 5.7 collective-permute-start.3
  436.7 3.2 all-to-all-start
  439.9 5.1 all-to-all-done
  445.2 19.9 %all-gather.2.cloned.1.call-done = f32[2048,256]{1,0:T(8,128)} async-done(((f32[512,256]{1,0:T(8,128)}), f32[2048,256]{1,0:T(8,128)}) %all-gather.2.cloned.1.call-update) | async-done | bytes 2097168 | tf_op jit(solution)/shard_map/all_gather | solution.py:36
  466.4 1.6 broadcast_select_fusion
  467.9 315.1 %custom-call.22 = f32[16,2,1,128,128]{3,4,2,1,0:T(8,128)S(1)} custom-call(f32[16,2,1,128,128]{4,3,2,1,0:T(8,128)} %broadcast_select_fusion), custom_call_target="InvertDiagBlocksLowerTriangular" | custom-call | tf_op jit(solution)/shard_map/triangular_solve | solution.py:50
  783.1 3.8 fusion.5
  786.9 3.7 fusion.38
  791.8 4.4 all-to-all-start.1
  799.8 1.8 copy.96
  801.6 10.0 %all-to-all-done.1 = bf16[16,2,128,128]{2,3,1,0:T(8,128)(2,1)} async-done(((bf16[16,2,128,128]{2,3,1,0:T(8,128)(2,1)}), bf16[16,2,128,128]{2,3,1,0:T(8,128)(2,1)}, u32[]{:S(2)}, u32[]{:S(2)}) %all-to-all-start.1) | async-done | bytes 1048608 | tf_op jit(solution)/shard_map/all_to_all | solution.py:86
  811.6 2.5 copy.82
  817.5 1.8 convolution_convert_fusion.1
  820.9 24.3 %custom-call.23 = f32[2,128,128]{2,1,0:T(8,128)S(1)} custom-call(f32[2,128,128]{2,1,0:T(8,128)} %fusion.26), custom_call_target="Cholesky" | custom-call | tf_op jit(solution)/shard_map/jit(cholesky)/cholesky | solution.py:41
  845.5 19.7 %custom-call.25 = f32[2,1,128,128]{2,3,1,0:T(8,128)S(1)} custom-call(f32[2,1,128,128]{3,2,1,0:T(8,128)S(1)} %get-tuple-element.10), custom_call_target="InvertDiagBlocksLowerTriangular" | custom-call | tf_op jit(solution)/shard_map/triangular_solve | solution.py:42
  865.6 99.1 %custom-call.24 = f32[2,5,1,128,128]{3,4,2,1,0:T(8,128)} custom-call(f32[2,5,1,128,128]{4,3,2,1,0:T(8,128)S(1)} %broadcast_select_fusion.1), custom_call_target="InvertDiagBlocksLowerTriangular" | custom-call | tf_op jit(solution)/shard_map/triangular_solve | solution.py:50
  964.7 1.8 fusion.16
  (65 shorter events, 20.0 us)
Async XLA Ops:
  7.2 5.4 copy-start.6
  7.2 422.8 %reduce-scatter.2.cloned.1.call-start = ((), (), s32[]{:S(2)}) async-start(), calls=%async_computation.3 | async-start | bytes 2621440 | tf_op jit(solution)/shard_map/reduce_scatter | solution.py:35
  8.6 15.6 %collective-permute-start = (bf16[5,256,256]{2,1,0:T(8,128)(2,1)S(1)}, bf16[5,256,256]{2,1,0:T(8,128)(2,1)S(1)}, u32[]{:S(2)}, u32[]{:S(2)}) collective-permute-start(bf16[5,256,256]{2,1,0:T(8,128)(2,1)S(1)} %get-tuple-element.14), channel_id=1, source_target_pairs={{0,4},{4,8},{8,12},{12,16},{16,20},{20,24},{24,28},{28,32},{32,36}... | collective-permute-start | bytes 1966088 | tf_op jit(solution)/shard_map/ppermute | solution.py:17
  10.2 16.3 %collective-permute-start.1 = (bf16[5,256,256]{2,1,0:T(8,128)(2,1)S(1)}, bf16[5,256,256]{2,1,0:T(8,128)(2,1)}, u32[]{:S(2)}, u32[]{:S(2)}) collective-permute-start(bf16[5,256,256]{2,1,0:T(8,128)(2,1)S(1)} %get-tuple-element.15), channel_id=1, source_target_pairs={{4,0},{8,4},{12,8},{16,12},{20,16},{24,20},{28,24},{32,28},{36,32}... | collective-permute-start | bytes 1966088 | tf_op jit(solution)/shard_map/ppermute | solution.py:18
  24.2 0.8 copy-start.5
  31.4 4.9 copy-start.1
  37.6 3.2 copy-start
  40.8 2.0 copy-start.2
  395.2 34.7 %copy-start.3 = (bf16[2,256,256]{2,1,0:T(8,128)(2,1)S(1)}, bf16[2,256,256]{2,1,0:T(8,128)(2,1)}, u32[]{:S(2)}) copy-start(bf16[2,256,256]{2,1,0:T(8,128)(2,1)} %param.6) | copy-start | bytes 786436
  395.2 69.8 %all-gather.2.cloned.1.call-start = ((), (), s32[]{:S(2)}) async-start(), calls=%async_computation.4 | async-start | bytes 2621440 | tf_op jit(solution)/shard_map/all_gather | solution.py:36
  430.0 366.2 %collective-permute-start.2 = (bf16[2,256,256]{2,1,0:T(8,128)(2,1)S(1)}, bf16[2,256,256]{2,1,0:T(8,128)(2,1)S(1)}, u32[]{:S(2)}, u32[]{:S(2)}) collective-permute-start(bf16[2,256,256]{2,1,0:T(8,128)(2,1)S(1)} %copy-done.3), channel_id=1, source_target_pairs={{0,1},{1,2},{2,3},{3,4},{4,5},{5,6},{6,7},{7,8},{8,9},{9,10},{10,1... | collective-permute-start | bytes 786440 | tf_op jit(solution)/shard_map/ppermute | solution.py:17
  430.3 368.0 %collective-permute-start.3 = (bf16[2,256,256]{2,1,0:T(8,128)(2,1)S(1)}, bf16[2,256,256]{2,1,0:T(8,128)(2,1)S(1)}, u32[]{:S(2)}, u32[]{:S(2)}) collective-permute-start(bf16[2,256,256]{2,1,0:T(8,128)(2,1)S(1)} %copy-done.3), channel_id=1, source_target_pairs={{1,0},{2,1},{3,2},{4,3},{5,4},{6,5},{7,6},{8,7},{9,8},{10,9},{11,1... | collective-permute-start | bytes 786440 | tf_op jit(solution)/shard_map/ppermute | solution.py:18
  436.7 8.4 all-to-all-start
  783.1 3.8 copy-start.4
  791.8 19.8 %all-to-all-start.1 = ((bf16[16,2,128,128]{2,3,1,0:T(8,128)(2,1)}), bf16[16,2,128,128]{2,3,1,0:T(8,128)(2,1)}, u32[]{:S(2)}, u32[]{:S(2)}) async-start(bf16[16,2,128,128]{2,3,1,0:T(8,128)(2,1)} %copy.81), calls=%async_computation.2 | async-start | bytes 2097152 | tf_op jit(solution)/shard_map/all_to_all | solution.py:86
Sparse Core Ops, SparseCore 0:
  395.4 34.5 reduce-scatter.1
  431.9 33.1 all-gather.1
where the time goes:
time: 986 us; the launch traced here: 975 us
  other arithmetic  813 us (82%)
  waiting for transfers between devices  82.6 us (8%)
  local copies, waits for them, and re-layouts  24.5 us (2%)
  matrix products  23 us (2%)
  starting transfers between devices  17.7 us (2%)
  between operations  14.7 us (1%)
    another operation x5, other arithmetic, reduce_rows(): lax.linalg.triangular_solve(widened, rotated[..., :spare_size, spare_size...  416 us
    another operation x7, other arithmetic, eliminate(): factor = jnp.linalg.cholesky(0.5 * (corner + jnp.swapaxes(corner, -1, -2)))  212 us
    another operation x4, other arithmetic, eliminate(): lax.linalg.triangular_solve(factor, rotated[..., :spare_size, spare_size:...  178 us
    reduce_scatter x1, waiting for transfers between devices, spread(): own = lax.psum_scatter(padded, axis, scatter_dimension=0, tiled=True)  34.6 us
    all_gather x1, waiting for transfers between devices, spread(): lax.all_gather(own, axis, axis=0, tiled=True)[:len(lines)]  19.9 us
  transfers between devices with their start and end apart: 8, of which 6 were waited for; matrix products, arithmetic and copies ran while one was open for 34% of the time, Pallas kernels for 0%

commit v1 on v0

v1 whole, which is shorter than its diff:
```python
import functools

import jax
import jax.numpy as jnp
from jax import lax
from jax.experimental import pallas as pl
from jax.experimental.pallas import tpu as pltpu
from jax.sharding import PartitionSpec as P

BLK = 256
RANK = 128
PANEL = 16
BF = jnp.bfloat16
F32 = jnp.float32


def mm(a, b):
    return lax.dot_general(a, b, (((1,), (0,)), ((), ())), preferred_element_type=F32)


def mm_t(a, b):
    return lax.dot_general(a, b, (((0,), (0,)), ((), ())), preferred_element_type=F32)


def split3(x):
    high = x.astype(BF)
    rest = x - high.astype(F32)
    mid = rest.astype(BF)
    low = (rest - mid.astype(F32)).astype(BF)
    return high, mid, low


def mm_exact(a, b):
    ah, am, al = split3(a)
    bh, bm, bl = split3(b)
    left = jnp.concatenate([ah, ah, am, ah, am, al], axis=1)
    right = jnp.concatenate([bh, bm, bh, bl, bm, bh], axis=0)
    return mm(left, right)


def mm_exact_t(a, b):
    ah, am, al = split3(a)
    bh, bm, bl = split3(b)
    left = jnp.concatenate([ah, ah, am, ah, am, al], axis=0)
    right = jnp.concatenate([bh, bm, bh, bl, bm, bh], axis=0)
    return mm_t(left, right)


def sweep_panel(panel, start):
    lane = lax.broadcasted_iota(jnp.int32, panel.shape, 2)
    sub = lax.broadcasted_iota(jnp.int32, panel.shape, 1)
    for step in range(PANEL):
        here = lane == start + step
        column = jnp.broadcast_to(panel[:, :, start + step : start + step + 1], panel.shape)
        pivot = column[:, step : step + 1]
        row = jnp.where(here[:, :1], 1.0, panel[:, step : step + 1]) / pivot
        rest = jnp.where(here, 0.0, panel) - column * row
        panel = jnp.where(sub == step, row, rest)
    return panel


def sweep(matrix_ref, count, group):
    order = matrix_ref.shape[-1]
    lane = lax.broadcasted_iota(jnp.int32, (order, order), 1)
    lane_panel = lax.broadcasted_iota(jnp.int32, (PANEL, order), 1)
    for start in range(0, order, PANEL):
        for first in range(0, count, group):
            rows = matrix_ref[first : first + group, start : start + PANEL, :]
            swept = sweep_panel(rows, start)
            inside = (lane >= start) & (lane < start + PANEL)
            inside_panel = (lane_panel >= start) & (lane_panel < start + PANEL)
            for leaf in range(group):
                signed = jnp.where(inside_panel, -swept[leaf], swept[leaf])
                update = mm_exact_t(rows[leaf], signed)
                matrix_ref[first + leaf] = jnp.where(inside, 0.0, matrix_ref[first + leaf]) - update
                matrix_ref[first + leaf, start : start + PANEL, :] = signed


def leaf_gain_kernel(near_ref, base_ref, gain_ref, matrix_ref, right_ref):
    count = near_ref.shape[0]

    @pl.loop(0, count)
    def _(leaf):
        base = base_ref[leaf]
        turned = mm(near_ref[leaf], base).astype(BF)
        rotated = mm_t(base[:, :RANK], turned)
        corner = rotated[:, :RANK]
        matrix_ref[leaf] = 0.5 * (corner + corner.T)
        right_ref[leaf] = rotated[:, RANK:]

    sweep(matrix_ref, count, 8)

    @pl.loop(0, count)
    def _(leaf):
        gain_ref[leaf] = (-mm_exact(right_ref[leaf].T, matrix_ref[leaf])).astype(BF)


def rotate_kernel(place_ref, near_ref, base_ref, wide_ref, right_ref, low_ref):
    count = near_ref.shape[0]

    @pl.loop(0, count)
    def _(leaf):
        base = base_ref[leaf]
        turned = [
            mm(near_ref[leaf, slot], wide_ref[place_ref[leaf, slot]]).astype(BF)
            for slot in range(2)
        ]
        rotated = mm_t(base, jnp.concatenate(turned, axis=1))
        for slot in range(2):
            right_ref[leaf, slot] = rotated[:RANK, slot * RANK : (slot + 1) * RANK]
            low_ref[leaf, slot] = rotated[RANK:, slot * RANK : (slot + 1) * RANK]


def leaf_skeleton_kernel(right_ref, low_ref, gain_ref, skeleton_ref, packed_ref):
    count = right_ref.shape[0]

    @pl.loop(0, count)
    def _(leaf):
        gain = gain_ref[leaf]
        for slot in range(2):
            block = low_ref[leaf, slot] - mm(gain, right_ref[leaf, slot].astype(BF))
            skeleton_ref[leaf, slot] = block
            packed_ref[leaf, slot] = block.astype(BF)


def upper_kernel(target_ref, block_ref, base_ref, before_ref, after_ref, out_ref,
                 merged_ref, matrix_ref, right_ref, low_ref):
    parents = base_ref.shape[0]
    merged_ref[...] = jnp.zeros_like(merged_ref)
    for leaf in range(2 * parents):
        for slot in range(8):
            place = (leaf // 2) * 10 + target_ref[leaf, slot]
            rows = slice((leaf % 2) * RANK, (leaf % 2 + 1) * RANK)
            merged_ref[place, rows, :] = block_ref[leaf, slot]
    for p in range(parents):
        base = base_ref[p]
        for d in range(5):
            left = jnp.concatenate([merged_ref[p * 10 + 2 * d], merged_ref[p * 10 + 2 * d + 1]], axis=1)
            q = p + d - 2
            if d == 2:
                partner = base
            elif q < 0:
                partner = before_ref[q + parents]
            elif q >= parents:
                partner = after_ref[q - parents]
            else:
                partner = base_ref[q, :, RANK:]
            mixed = mm(left, partner).astype(BF)
            lifted = mm_t(base, mixed)
            if d == 2:
                corner = lifted[:RANK, :RANK]
                matrix_ref[p] = 0.5 * (corner + corner.T)
                lifted = lifted[:, RANK:]
            right_ref[p, d] = lifted[:RANK]
            low_ref[p, d] = lifted[RANK:]
    sweep(matrix_ref, parents, parents)
    for p in range(parents):
        gain = mm_exact(right_ref[p, 2].T, matrix_ref[p])
        for d in range(5):
            out_ref[p, d] = low_ref[p, d] + mm(gain.astype(BF), right_ref[p, d].astype(BF))


VM = pl.BlockSpec(memory_space=pltpu.VMEM)
SM = pl.BlockSpec(memory_space=pltpu.SMEM)
PARAMS = pltpu.CompilerParams(vmem_limit_bytes=48 * 1024 * 1024)


def shaped(shape, dtype):
    return jax.ShapeDtypeStruct(shape, dtype)


def leaf_gain(near, base):
    count = near.shape[0]
    return pl.pallas_call(
        leaf_gain_kernel,
        grid=(1,),
        in_specs=[pl.BlockSpec((count, None, BLK, BLK), lambda g: (0, 0, 0, 0)), VM],
        out_specs=VM,
        out_shape=shaped((count, RANK, RANK), BF),
        scratch_shapes=[pltpu.VMEM((count, RANK, RANK), F32)] * 2,
        compiler_params=PARAMS,
        name="leaf_gain",
    )(near, base)


def rotate(place, near, base, wide):
    count = near.shape[0]
    return pl.pallas_call(
        rotate_kernel,
        in_specs=[SM, VM, VM, VM],
        out_specs=[VM, VM],
        out_shape=[shaped((count, 2, RANK, RANK), F32)] * 2,
        compiler_params=PARAMS,
        name="rotate",
    )(place, near, base, wide)


def leaf_skeleton(right, low, gain):
    return pl.pallas_call(
        leaf_skeleton_kernel,
        in_specs=[VM] * 3,
        out_specs=[VM, VM],
        out_shape=[shaped(right.shape, F32), shaped(right.shape, BF)],
        compiler_params=PARAMS,
        name="leaf_skeleton",
    )(right, low, gain)


def upper(target, blocks, base, before, after):
    parents = base.shape[0]
    return pl.pallas_call(
        upper_kernel,
        in_specs=[SM] + [VM] * 4,
        out_specs=VM,
        out_shape=shaped((parents, 5, RANK, RANK), F32),
        scratch_shapes=[
            pltpu.VMEM((parents * 10, 2 * RANK, RANK), BF),
            pltpu.VMEM((parents, RANK, RANK), F32),
            pltpu.VMEM((parents, 5, RANK, RANK), F32),
            pltpu.VMEM((parents, 5, RANK, RANK), F32),
        ],
        compiler_params=PARAMS,
        name="upper",
    )(target, blocks, base, before, after)


def halo(last, initial, axis):
    count = lax.axis_size(axis)
    up = [(i, (i + 1) % count) for i in range(count)]
    down = [(j, i) for i, j in up]
    return lax.ppermute(last, axis, up), lax.ppermute(initial, axis, down)


def per_device(near_blocks, leaf_bases, upper_bases, neighbours):
    count = near_blocks.shape[0]
    total = count * lax.axis_size(("node", "trow"))
    first_leaf = lax.axis_index(("node", "trow")) * count
    skeleton_bases = leaf_bases[:, :, RANK:]
    before, after = halo(skeleton_bases[count - 4 :], skeleton_bases[:4], ("node", "trow"))
    upper_half = upper_bases[:, :, RANK:]
    upper_before, upper_after = halo(upper_half, upper_half, ("node", "trow", "tcol"))
    leaf_ids = first_leaf + jnp.arange(count, dtype=jnp.int32)
    target = 2 * ((neighbours // 2 - leaf_ids[:, None] // 2 + 2) % (total // 2)) + neighbours % 2
    arrived_target = lax.all_to_all(target, "tcol", split_axis=0, concat_axis=1, tiled=True)
    gain = leaf_gain(near_blocks, leaf_bases)
    sent = [lax.ppermute(gain, "tcol", [(0, j)]) for j in (1, 2, 3)]
    wide = jnp.concatenate([before, skeleton_bases, after], axis=0)
    place = (neighbours - first_leaf + total // 2) % total - total // 2 + 4
    right, low = rotate(place, near_blocks, leaf_bases, wide)
    mine = lax.axis_index("tcol")
    for j in (1, 2, 3):
        gain = jnp.where(mine == j, sent[j - 1], gain)
    skeleton, packed = leaf_skeleton(right, low, gain)
    arrived = lax.all_to_all(packed, "tcol", split_axis=0, concat_axis=1, tiled=True)
    upper_skeleton = upper(arrived_target, arrived, upper_bases, upper_before, upper_after)
    return (skeleton, upper_skeleton)


def solution(mesh):
    return jax.shard_map(
        per_device,
        mesh=mesh,
        in_specs=(
            P(("node", "trow"), "tcol", None, None),
            P(("node", "trow"), None, None),
            P(("node", "trow", "tcol"), None, None),
            P(("node", "trow"), "tcol"),
        ),
        out_specs=(
            P(("node", "trow"), "tcol", None, None),
            P(("node", "trow", "tcol"), None, None, None),
        ),
        check_vma=False,
    )
```

time: 986 us -> 102 us (0.10); the launches traced: 975 us -> 101 us
  other arithmetic: 813 us -> 1.35 us
  waiting for transfers between devices: 82.6 us -> 13.6 us
  Pallas kernels: 0 us -> 57.4 us
  matrix products: 23 us -> 0 us
  local copies, waits for them, and re-layouts: 24.5 us -> 3.51 us
  between operations: 14.7 us -> 0.79 us
    another operation x16 -> x0, other arithmetic: 806 us -> none  [the longest x5 416 us: reduce_rows(): lax.linalg.triangular_solve(widened, rotated[..., :spare_size, spare_size...]
    pallas_call x0 -> x4, Pallas kernels: none -> 57.4 us  [the longest x1 28.2 us: leaf_gain(): pl.pallas_call(leaf_gain_kernel, grid=(1,), in_specs=[pl.BlockSpec((count...]
    reduce_scatter x1 -> x0, waiting for transfers between devices: 34.6 us -> none  [spread(): own = lax.psum_scatter(padded, axis, scatter_dimension=0, tiled=True)]
    all_gather x1 -> x0, waiting for transfers between devices: 19.9 us -> none  [spread(): lax.all_gather(own, axis, axis=0, tiled=True)[:len(lines)]]
    dot_general x7 -> x0, matrix products: 13.9 us -> none  [the longest x1 4.9 us: per_device(): jnp.einsum('lkab,lkbc->lkac', near_blocks, partner, preferred_element_typ...]
    ppermute x4 -> x7, waiting for transfers between devices: 12.8 us -> 1.19 us  [the longest x4 1.19 us: halo(): return (lax.ppermute(last, axis, up), lax.ppermute(initial, axis, down))]
  transfers between devices with their start and end apart: 8 -> 9, of which waited for: 6 -> 3; matrix products, arithmetic and copies ran while one was open for 34% -> 3% of each run, Pallas kernels for 0% -> 14%
where the time goes in v1:
time: 102 us; the launch traced here: 101 us
  Pallas kernels  57.4 us (56%)
  starting transfers between devices  24.6 us (24%)
  waiting for transfers between devices  13.6 us (13%)
  local copies, waits for them, and re-layouts  3.51 us (3%)
  other arithmetic  1.35 us (1%)
    pallas_call x1, Pallas kernels, leaf_gain(): pl.pallas_call(leaf_gain_kernel, grid=(1,), in_specs=[pl.BlockSpec((count...  28.2 us
    pallas_call x1, Pallas kernels, upper(): pl.pallas_call(upper_kernel, in_specs=[SM] + [VM] * 4, out_specs=VM, out_...  15.1 us
    all_to_all x1, waiting for transfers between devices, per_device(): lax.all_to_all(packed, 'tcol', split_axis=0, concat_axis=1, tiled=True)  12.4 us
    ppermute x4, starting transfers between devices, halo(): return (lax.ppermute(last, axis, up), lax.ppermute(initial, axis, down))  9.9 us
    pallas_call x1, Pallas kernels, rotate(): pl.pallas_call(rotate_kernel, in_specs=[SM, VM, VM, VM], out_specs=[VM, V...  9.81 us
    ppermute x3, starting transfers between devices, per_device(): sent = [lax.ppermute(gain, 'tcol', [(0, j)]) for j in (1, 2, 3)]  7.74 us
    pallas_call x1, Pallas kernels, leaf_skeleton(): pl.pallas_call(leaf_skeleton_kernel, in_specs=[VM] * 3, out_specs=[VM, VM...  4.23 us
    all_to_all x1, starting transfers between devices, per_device(): lax.all_to_all(packed, 'tcol', split_axis=0, concat_axis=1, tiled=True)  3.77 us
  transfers between devices with their start and end apart: 9, of which 3 were waited for; matrix products, arithmetic and copies ran while one was open for 3% of the time, Pallas kernels for 14%

profile of v1, /device:TPU:96, one launch (start us, length us, event | category | flops | bytes accessed | tf_op | source)
XLA Modules:
  0.0 101.3 jit_solution(7958415568462215842)
XLA Ops:
  0.6 0.0 copy-start
  0.6 1.6 %copy-done = bf16[16,256,256]{2,1,0:T(8,128)(2,1)S(1)} copy-done((bf16[16,256,256]{2,1,0:T(8,128)(2,1)S(1)}, bf16[16,256,256]{2,1,0:T(8,128)(2,1)}, u32[]{:S(2)}) %copy-start) | copy-done | bytes 2097176
  2.2 28.2 %leaf_gain.1 = bf16[16,128,128]{2,1,0:T(8,128)(2,1)S(1)} custom-call(bf16[16,2,256,256]{3,2,1,0:T(8,128)(2,1)} %near_ref.3, bf16[16,256,256]{2,1,0:T(8,128)(2,1)S(1)} %copy-done), custom_call_target="tpu_custom_call" | custom-call | tf_op jit(solution)/shard_map/leaf_gain/pallas_call | solution.py:174
  30.4 0.0 slice-start
  30.5 5.1 %collective-permute-start.2 = (bf16[16,128,128]{2,1,0:T(8,128)(2,1)S(1)}, bf16[16,128,128]{2,1,0:T(8,128)(2,1)S(1)}, u32[]{:S(2)}, u32[]{:S(2)}) collective-permute-start(bf16[16,128,128]{2,1,0:T(8,128)(2,1)S(1)} %leaf_gain.1), channel_id=1, source_target_pairs={{0,3},{4,7},{8,11},{12,15},{16,19},{20,23},{24,27},{28,31},{32,35}... | collective-permute-start | bytes 1572872 | tf_op jit(solution)/shard_map/ppermute | solution.py:246
  35.6 1.3 %collective-permute-start.3 = (bf16[16,128,128]{2,1,0:T(8,128)(2,1)S(1)}, bf16[16,128,128]{2,1,0:T(8,128)(2,1)S(1)}, u32[]{:S(2)}, u32[]{:S(2)}) collective-permute-start(bf16[16,128,128]{2,1,0:T(8,128)(2,1)S(1)} %leaf_gain.1), channel_id=1, source_target_pairs={{0,2},{4,6},{8,10},{12,14},{16,18},{20,22},{24,26},{28,30},{32,34}... | collective-permute-start | bytes 1572872 | tf_op jit(solution)/shard_map/ppermute | solution.py:246
  36.9 1.3 %collective-permute-start.4 = (bf16[16,128,128]{2,1,0:T(8,128)(2,1)S(1)}, bf16[16,128,128]{2,1,0:T(8,128)(2,1)S(1)}, u32[]{:S(2)}, u32[]{:S(2)}) collective-permute-start(bf16[16,128,128]{2,1,0:T(8,128)(2,1)S(1)} %leaf_gain.1), channel_id=1, source_target_pairs={{0,1},{4,5},{8,9},{12,13},{16,17},{20,21},{24,25},{28,29},{32,33},... | collective-permute-start | bytes 1572872 | tf_op jit(solution)/shard_map/ppermute | solution.py:246
  38.2 0.9 fusion.8
  39.1 1.5 %collective-permute-start = (bf16[4,256,128]{2,1,0:T(8,128)(2,1)}, bf16[4,256,128]{2,1,0:T(8,128)(2,1)S(1)}, u32[]{:S(2)}, u32[]{:S(2)}) collective-permute-start(bf16[4,256,128]{2,1,0:T(8,128)(2,1)} %get-tuple-element.10), channel_id=1, source_target_pairs={{0,4},{4,8},{8,12},{12,16},{16,20},{20,24},{24,28},{28,32},{32,36}... | collective-permute-start | bytes 786440 | tf_op jit(solution)/shard_map/ppermute | solution.py:231
  40.6 2.4 %collective-permute-start.1 = (bf16[4,256,128]{2,1,0:T(8,128)(2,1)}, bf16[4,256,128]{2,1,0:T(8,128)(2,1)}, u32[]{:S(2)}, u32[]{:S(2)}) collective-permute-start(bf16[4,256,128]{2,1,0:T(8,128)(2,1)} %get-tuple-element.11), channel_id=1, source_target_pairs={{4,0},{8,4},{12,8},{16,12},{20,16},{24,20},{28,24},{32,28},{36,32}... | collective-permute-start | bytes 786440 | tf_op jit(solution)/shard_map/ppermute | solution.py:231
  43.0 0.1 copy.27
  43.1 0.1 fusion.6
  43.1 0.7 copy.32
  43.8 3.2 %all-to-all-start = ((s32[4,4,2]{1,2,0:T(2,128)}), s32[4,4,2]{1,2,0:T(2,128)S(1)}, u32[]{:S(2)}, u32[]{:S(2)}) async-start(s32[4,4,2]{1,2,0:T(2,128)} %copy.32), calls=%async_computation | async-start | bytes 8192 | tf_op jit(solution)/shard_map/all_to_all | solution.py:244
  47.1 0.1 copy.26
  47.2 0.1 collective-permute-done
  47.3 1.1 %collective-permute-done.1 = bf16[4,256,128]{2,1,0:T(8,128)(2,1)} collective-permute-done((bf16[4,256,128]{2,1,0:T(8,128)(2,1)}, bf16[4,256,128]{2,1,0:T(8,128)(2,1)}, u32[]{:S(2)}, u32[]{:S(2)}) %collective-permute-start.1) | collective-permute-done | bytes 262176 | tf_op jit(solution)/shard_map/ppermute | solution.py:231
  48.4 1.1 %pad_maximum_fusion.wide_ref = bf16[24,256,128]{2,1,0:T(8,128)(2,1)S(1)} fusion(bf16[4,256,128]{2,1,0:T(8,128)(2,1)} %collective-permute-done.1, bf16[16,256,128]{2,1,0:T(8,128)(2,1)S(1)} %slice-done, bf16[4,256,128]{2,1,0:T(8,128)(2,1)S(1)} %collective-permute-done), kind=kLoop, calls=%fused_computation | loop fusion | flops 1572864 | bytes 3145728 | tf_op jit(solution)/shard_map/concatenate | solution.py:247
  49.5 9.8 %rotate.1 = (f32[16,2,128,128]{3,2,1,0:T(8,128)S(1)}, f32[16,2,128,128]{3,2,1,0:T(8,128)S(1)}) custom-call(s32[16,2]{1,0:T(8,128)S(1)} %fusion.1.place_ref, bf16[16,2,256,256]{3,2,1,0:T(8,128)(2,1)} %near_ref.3, bf16[16,256,256]{2,1,0:T(8,128)(2,1)} %base_ref.4, bf16[24,256,128]{2,1,0:T(8,128)(2,1)S(1)} %pad_maximum_fusion.wide_ref), custom_call_target="tpu_custom_call" | custom-call | tf_op jit(solution)/shard_map/rotate/pallas_call | solution.py:188
  59.4 0.0 collective-permute-done.3
  59.4 0.0 collective-permute-done.4
  59.4 0.1 select_select_fusion.gain_ref
  59.5 4.2 %leaf_skeleton.1 = (f32[16,2,128,128]{3,2,1,0:T(8,128)}, bf16[16,2,128,128]{3,2,1,0:T(8,128)(2,1)}) custom-call(f32[16,2,128,128]{3,2,1,0:T(8,128)S(1)} %get-tuple-element.6.right_ref, f32[16,2,128,128]{3,2,1,0:T(8,128)S(1)} %get-tuple-element.7.low_ref, bf16[16,128,128]{2,1,0:T(8,128)(2,1)S(1)} %select_select_fusion.gain_ref), custom_call_target="tpu_custom_call" | custom-call | tf_op jit(solution)/shard_map/leaf_skeleton/pallas_call | solution.py:199
  63.7 0.0 all-to-all-done
  63.7 3.8 %all-to-all-start.1 = ((bf16[16,2,128,128]{3,2,1,0:T(8,128)(2,1)}), bf16[16,2,128,128]{3,2,1,0:T(8,128)(2,1)S(1)}, u32[]{:S(2)}, u32[]{:S(2)}) async-start(bf16[16,2,128,128]{3,2,1,0:T(8,128)(2,1)} %get-tuple-element.9), calls=%async_computation.1 | async-start | bytes 2097152 | tf_op jit(solution)/shard_map/all_to_all | solution.py:254
  67.5 2.3 %collective-permute-start.5 = (bf16[2,256,128]{2,1,0:T(8,128)(2,1)S(1)}, bf16[2,256,128]{2,1,0:T(8,128)(2,1)S(1)}, u32[]{:S(2)}, u32[]{:S(2)}) collective-permute-start(bf16[2,256,128]{2,1,0:T(8,128)(2,1)S(1)} %slice.17), channel_id=1, source_target_pairs={{0,1},{1,2},{2,3},{3,4},{4,5},{5,6},{6,7},{7,8},{8,9},{9,10},{10,1... | collective-permute-start | bytes 393224 | tf_op jit(solution)/shard_map/ppermute | solution.py:231
  69.8 3.7 %collective-permute-start.6 = (bf16[2,256,128]{2,1,0:T(8,128)(2,1)S(1)}, bf16[2,256,128]{2,1,0:T(8,128)(2,1)S(1)}, u32[]{:S(2)}, u32[]{:S(2)}) collective-permute-start(bf16[2,256,128]{2,1,0:T(8,128)(2,1)S(1)} %slice.17), channel_id=1, source_target_pairs={{1,0},{2,1},{3,2},{4,3},{5,4},{6,5},{7,6},{8,7},{9,8},{10,9},{11,1... | collective-permute-start | bytes 393224 | tf_op jit(solution)/shard_map/ppermute | solution.py:231
  73.6 0.1 copy.34.target_ref
  73.6 12.4 %all-to-all-done.1 = bf16[16,2,128,128]{3,2,1,0:T(8,128)(2,1)S(1)} async-done(((bf16[16,2,128,128]{3,2,1,0:T(8,128)(2,1)}), bf16[16,2,128,128]{3,2,1,0:T(8,128)(2,1)S(1)}, u32[]{:S(2)}, u32[]{:S(2)}) %all-to-all-start.1) | async-done | bytes 1048608 | tf_op jit(solution)/shard_map/all_to_all | solution.py:254
  86.1 0.1 copy.33
  86.1 0.0 collective-permute-done.5.before_ref
  86.2 15.1 %upper.1 = f32[2,5,128,128]{3,2,1,0:T(8,128)} custom-call(s32[4,8]{1,0:T(4,128)S(1)} %copy.34.target_ref, bf16[4,8,128,128]{3,2,1,0:T(8,128)(2,1)S(1)} %bitcast.8, bf16[2,256,256]{2,1,0:T(8,128)(2,1)S(1)} %copy-done.1, bf16[2,256,128]{2,1,0:T(8,128)(2,1)S(1)} %collective-permute-done.5.before_ref, bf16[2,256,128]{2,1,0:T(8,128)(2,1)S(1)} %collective-permute-done.6.after_ref), custom_call_target="tpu_custom_call" | custom-call | tf_op jit(solution)/shard_map/upper/pallas_call | solution.py:211
  (11 shorter events, 0.1 us)
Async XLA Ops:
  0.6 1.6 %copy-start = (bf16[16,256,256]{2,1,0:T(8,128)(2,1)S(1)}, bf16[16,256,256]{2,1,0:T(8,128)(2,1)}, u32[]{:S(2)}) copy-start(bf16[16,256,256]{2,1,0:T(8,128)(2,1)} %base_ref.4) | copy-start | bytes 6291460
  2.2 40.7 %copy-start.2 = (s32[16,2]{0,1:T(2,128)S(1)}, s32[16,2]{0,1:T(2,128)}, u32[]{:S(2)}) copy-start(s32[16,2]{0,1:T(2,128)} %param.7) | copy-start | bytes 388
  30.4 18.0 %slice-start = ((bf16[16,256,256]{2,1,0:T(8,128)(2,1)}), bf16[16,256,128]{2,1,0:T(8,128)(2,1)S(1)}, s32[]{:S(2)}) async-start(bf16[16,256,256]{2,1,0:T(8,128)(2,1)} %base_ref.4), calls=%async_computation.2 | async-start | bytes 2097152 | tf_op jit(solution)/shard_map/slice | solution.py:238
  30.5 28.9 %collective-permute-start.2 = (bf16[16,128,128]{2,1,0:T(8,128)(2,1)S(1)}, bf16[16,128,128]{2,1,0:T(8,128)(2,1)S(1)}, u32[]{:S(2)}, u32[]{:S(2)}) collective-permute-start(bf16[16,128,128]{2,1,0:T(8,128)(2,1)S(1)} %leaf_gain.1), channel_id=1, source_target_pairs={{0,3},{4,7},{8,11},{12,15},{16,19},{20,23},{24,27},{28,31},{32,35}... | collective-permute-start | bytes 1572872 | tf_op jit(solution)/shard_map/ppermute | solution.py:246
  35.6 23.8 %collective-permute-start.3 = (bf16[16,128,128]{2,1,0:T(8,128)(2,1)S(1)}, bf16[16,128,128]{2,1,0:T(8,128)(2,1)S(1)}, u32[]{:S(2)}, u32[]{:S(2)}) collective-permute-start(bf16[16,128,128]{2,1,0:T(8,128)(2,1)S(1)} %leaf_gain.1), channel_id=1, source_target_pairs={{0,2},{4,6},{8,10},{12,14},{16,18},{20,22},{24,26},{28,30},{32,34}... | collective-permute-start | bytes 1572872 | tf_op jit(solution)/shard_map/ppermute | solution.py:246
  36.9 22.5 %collective-permute-start.4 = (bf16[16,128,128]{2,1,0:T(8,128)(2,1)S(1)}, bf16[16,128,128]{2,1,0:T(8,128)(2,1)S(1)}, u32[]{:S(2)}, u32[]{:S(2)}) collective-permute-start(bf16[16,128,128]{2,1,0:T(8,128)(2,1)S(1)} %leaf_gain.1), channel_id=1, source_target_pairs={{0,1},{4,5},{8,9},{12,13},{16,17},{20,21},{24,25},{28,29},{32,33},... | collective-permute-start | bytes 1572872 | tf_op jit(solution)/shard_map/ppermute | solution.py:246
  39.1 8.2 %collective-permute-start = (bf16[4,256,128]{2,1,0:T(8,128)(2,1)}, bf16[4,256,128]{2,1,0:T(8,128)(2,1)S(1)}, u32[]{:S(2)}, u32[]{:S(2)}) collective-permute-start(bf16[4,256,128]{2,1,0:T(8,128)(2,1)} %get-tuple-element.10), channel_id=1, source_target_pairs={{0,4},{4,8},{8,12},{12,16},{16,20},{20,24},{24,28},{28,32},{32,36}... | collective-permute-start | bytes 786440 | tf_op jit(solution)/shard_map/ppermute | solution.py:231
  40.6 7.8 %collective-permute-start.1 = (bf16[4,256,128]{2,1,0:T(8,128)(2,1)}, bf16[4,256,128]{2,1,0:T(8,128)(2,1)}, u32[]{:S(2)}, u32[]{:S(2)}) collective-permute-start(bf16[4,256,128]{2,1,0:T(8,128)(2,1)} %get-tuple-element.11), channel_id=1, source_target_pairs={{4,0},{8,4},{12,8},{16,12},{20,16},{24,20},{28,24},{32,28},{36,32}... | collective-permute-start | bytes 786440 | tf_op jit(solution)/shard_map/ppermute | solution.py:231
  43.8 19.9 %all-to-all-start = ((s32[4,4,2]{1,2,0:T(2,128)}), s32[4,4,2]{1,2,0:T(2,128)S(1)}, u32[]{:S(2)}, u32[]{:S(2)}) async-start(s32[4,4,2]{1,2,0:T(2,128)} %copy.32), calls=%async_computation | async-start | bytes 8192 | tf_op jit(solution)/shard_map/all_to_all | solution.py:244
  63.7 3.8 %copy-start.1 = (bf16[2,256,256]{2,1,0:T(8,128)(2,1)S(1)}, bf16[2,256,256]{2,1,0:T(8,128)(2,1)}, u32[]{:S(2)}) copy-start(bf16[2,256,256]{2,1,0:T(8,128)(2,1)} %base_ref.5) | copy-start | bytes 786436
  63.7 22.3 %all-to-all-start.1 = ((bf16[16,2,128,128]{3,2,1,0:T(8,128)(2,1)}), bf16[16,2,128,128]{3,2,1,0:T(8,128)(2,1)S(1)}, u32[]{:S(2)}, u32[]{:S(2)}) async-start(bf16[16,2,128,128]{3,2,1,0:T(8,128)(2,1)} %get-tuple-element.9), calls=%async_computation.1 | async-start | bytes 2097152 | tf_op jit(solution)/shard_map/all_to_all | solution.py:254
  67.5 18.6 %collective-permute-start.5 = (bf16[2,256,128]{2,1,0:T(8,128)(2,1)S(1)}, bf16[2,256,128]{2,1,0:T(8,128)(2,1)S(1)}, u32[]{:S(2)}, u32[]{:S(2)}) collective-permute-start(bf16[2,256,128]{2,1,0:T(8,128)(2,1)S(1)} %slice.17), channel_id=1, source_target_pairs={{0,1},{1,2},{2,3},{3,4},{4,5},{5,6},{6,7},{7,8},{8,9},{9,10},{10,1... | collective-permute-start | bytes 393224 | tf_op jit(solution)/shard_map/ppermute | solution.py:231
  69.8 16.3 %collective-permute-start.6 = (bf16[2,256,128]{2,1,0:T(8,128)(2,1)S(1)}, bf16[2,256,128]{2,1,0:T(8,128)(2,1)S(1)}, u32[]{:S(2)}, u32[]{:S(2)}) collective-permute-start(bf16[2,256,128]{2,1,0:T(8,128)(2,1)S(1)} %slice.17), channel_id=1, source_target_pairs={{1,0},{2,1},{3,2},{4,3},{5,4},{6,5},{7,6},{8,7},{9,8},{10,9},{11,1... | collective-permute-start | bytes 393224 | tf_op jit(solution)/shard_map/ppermute | solution.py:231

commit v2 on v1

v2 whole, which is shorter than its diff:
```python
import functools

import jax
import jax.numpy as jnp
from jax import lax
from jax.experimental import pallas as pl
from jax.experimental.pallas import tpu as pltpu
from jax.sharding import PartitionSpec as P

BLK = 256
RANK = 128
PANEL = 16
SHARE = 4
MESH = pl.DeviceIdType.MESH
BF = jnp.bfloat16
F32 = jnp.float32


def mm(a, b):
    return lax.dot_general(a, b, (((1,), (0,)), ((), ())), preferred_element_type=F32)


def mm_t(a, b):
    return lax.dot_general(a, b, (((0,), (0,)), ((), ())), preferred_element_type=F32)


def split3(x):
    high = x.astype(BF)
    rest = x - high.astype(F32)
    mid = rest.astype(BF)
    low = (rest - mid.astype(F32)).astype(BF)
    return high, mid, low


def mm_exact(a, b):
    ah, am, al = split3(a)
    bh, bm, bl = split3(b)
    left = jnp.concatenate([ah, ah, am, ah, am, al], axis=1)
    right = jnp.concatenate([bh, bm, bh, bl, bm, bh], axis=0)
    return mm(left, right)


def mm_exact_t(a, b):
    ah, am, al = split3(a)
    bh, bm, bl = split3(b)
    left = jnp.concatenate([ah, ah, am, ah, am, al], axis=0)
    right = jnp.concatenate([bh, bm, bh, bl, bm, bh], axis=0)
    return mm_t(left, right)


def sweep_panel(panel, start):
    lane = lax.broadcasted_iota(jnp.int32, panel.shape, 2)
    sub = lax.broadcasted_iota(jnp.int32, panel.shape, 1)
    for step in range(PANEL):
        here = lane == start + step
        column = jnp.broadcast_to(panel[:, :, start + step : start + step + 1], panel.shape)
        pivot = column[:, step : step + 1]
        row = jnp.where(here[:, :1], 1.0, panel[:, step : step + 1]) / pivot
        rest = jnp.where(here, 0.0, panel) - column * row
        panel = jnp.where(sub == step, row, rest)
    return panel


def sweep_panel_by_four(panel, start):
    parts = [panel[:, 8 * h : 8 * h + 8] for h in range(PANEL // 8)]
    shape = parts[0].shape
    lane = lax.broadcasted_iota(jnp.int32, (1,) + shape[1:], 2)
    sub = lax.broadcasted_iota(jnp.int32, (1,) + shape[1:], 1)

    def spread_row(x, row):
        return jnp.broadcast_to(x[:, row : row + 1], shape)

    for step in range(0, PANEL, 4):
        home, k = divmod(step, 8)
        s = start + step
        inside = (lane >= s) & (lane < s + 4)
        columns = [
            [jnp.broadcast_to(x[:, :, s + t : s + t + 1], shape) for x in parts] for t in range(4)
        ]
        e = {
            (i, j): spread_row(columns[j][home], k + i) for j in range(4) for i in range(j + 1)
        }
        r = [
            jnp.where(inside, jnp.where(lane == s + t, 1.0, 0.0), spread_row(parts[home], k + t))
            for t in range(4)
        ]
        first = 1.0 / (e[0, 0] * e[1, 1] - e[0, 1] * e[0, 1])

        def solve(p, q):
            return (e[1, 1] * p - e[0, 1] * q) * first, (e[0, 0] * q - e[0, 1] * p) * first

        u2, v2 = solve(e[0, 2], e[1, 2])
        u3, v3 = solve(e[0, 3], e[1, 3])
        s22 = e[2, 2] - (e[0, 2] * u2 + e[1, 2] * v2)
        s23 = e[2, 3] - (e[0, 2] * u3 + e[1, 2] * v3)
        s33 = e[3, 3] - (e[0, 3] * u3 + e[1, 3] * v3)
        second = 1.0 / (s22 * s33 - s23 * s23)
        t2 = r[2] - (u2 * r[0] + v2 * r[1])
        t3 = r[3] - (u3 * r[0] + v3 * r[1])
        n2 = (s33 * t2 - s23 * t3) * second
        n3 = (s22 * t3 - s23 * t2) * second
        m0, m1 = solve(r[0], r[1])
        n = [m0 - (u2 * n2 + u3 * n3), m1 - (v2 * n2 + v3 * n3), n2, n3]
        fresh = []
        for h, x in enumerate(parts):
            y = jnp.where(inside, 0.0, x) - (
                (columns[0][h] * n[0] + columns[1][h] * n[1])
                + (columns[2][h] * n[2] + columns[3][h] * n[3])
            )
            if h == home:
                for t in range(4):
                    y = jnp.where(sub == k + t, n[t], y)
            fresh.append(y)
        parts = fresh
    return jnp.concatenate(parts, axis=1)


def sweep(matrix_ref, swept_ref, panel_of):
    count, order = matrix_ref.shape[:2]
    lane = lax.broadcasted_iota(jnp.int32, (order, order), 1)
    lane_panel = lax.broadcasted_iota(jnp.int32, (count, PANEL, order), 2)
    for start in range(0, order, PANEL):
        rows = slice(start, start + PANEL)
        swept = panel_of(matrix_ref[:, rows, :], start)
        inside_panel = (lane_panel >= start) & (lane_panel < start + PANEL)
        swept_ref[...] = jnp.where(inside_panel, -swept, swept)

        @pl.loop(0, count, unroll=min(count, 8))
        def _(leaf):
            inside = (lane >= start) & (lane < start + PANEL)
            signed = swept_ref[leaf]
            update = mm_exact_t(matrix_ref[leaf, rows, :], signed)
            matrix_ref[leaf] = jnp.where(inside, 0.0, matrix_ref[leaf]) - update
            matrix_ref[leaf, rows, :] = signed


def exchange_kernel(place_ref, label_in_ref, near_ref, base_ref, upper_ref,
                    skeleton_ref, arrived_ref, label_ref, above_ref, below_ref,
                    wide_ref, gain_ref, right_ref, low_ref, packed_ref,
                    matrix_ref, corner_ref, swept_ref, near_sems, upper_sems, label_sems, gain_sems, block_sems):
    count = near_ref.shape[0]
    node, row, mine = lax.axis_index("node"), lax.axis_index("trow"), lax.axis_index("tcol")
    nodes, rows = lax.axis_size("node"), lax.axis_size("trow")
    line = node * rows + row
    lines = nodes * rows

    def at(line_of, col):
        return (line_of // rows, line_of % rows, col)

    next_line, last_line = (line + 1) % lines, (line + lines - 1) % lines
    order = line * SHARE + mine
    following, previous = (order + 1) % (lines * SHARE), (order + lines * SHARE - 1) % (lines * SHARE)
    after, before = at(next_line, mine), at(last_line, mine)
    upper_after = at(following // SHARE, following % SHARE)
    upper_before = at(previous // SHARE, previous % SHARE)
    mates = [at(line, (mine + off) % SHARE) for off in range(1, SHARE)]

    barrier = pltpu.get_barrier_semaphore()
    for device in [after, before, upper_after, upper_before] + mates:
        pl.semaphore_signal(barrier, inc=1, device_id=device, device_id_type=MESH)

    wide_ref[4 : 4 + count] = base_ref[:, :, RANK:]

    label_ref[mine] = label_in_ref[mine]
    pl.semaphore_wait(barrier, 4 + len(mates))

    def remote(src, dst, sems, index, device):
        return pltpu.make_async_remote_copy(
            src_ref=src, dst_ref=dst, send_sem=sems.at[(0,) + index], recv_sem=sems.at[(1,) + index],
            device_id=device, device_id_type=MESH,
        )

    half = pl.ds(RANK, RANK)
    near_copies = [
        remote(base_ref.at[pl.ds(count - 4, 4), :, half], wide_ref.at[pl.ds(0, 4)], near_sems, (0,), after),
        remote(base_ref.at[pl.ds(0, 4), :, half], wide_ref.at[pl.ds(4 + count, 4)], near_sems, (1,), before),
    ]
    for copy in near_copies:
        copy.start()

    def gain_copy(part, col):
        return remote(gain_ref.at[part], gain_ref.at[part], gain_sems, (part,), at(line, col))

    def pass_on(part):
        @pl.when((part < 2) & (mine < SHARE - 1))
        def _():
            gain_copy(part, (mine + 1) % SHARE).start()

        @pl.when((part >= 2) & (mine != 1))
        def _():
            gain_copy(part, (mine + SHARE - 1) % SHARE).start()

    upper_copies = [
        remote(upper_ref.at[:, :, half], above_ref, upper_sems, (0,), upper_after),
        remote(upper_ref.at[:, :, half], below_ref, upper_sems, (1,), upper_before),
    ]
    label_copies = [
        remote(label_in_ref.at[(mine + off) % SHARE], label_ref.at[mine], label_sems, (off - 1,), mates[off - 1])
        for off in range(1, SHARE)
    ]
    for copy in upper_copies + label_copies:
        copy.start()

    @pl.when(mine == 0)
    def _():
        @pl.loop(0, count, unroll=4)
        def _(leaf):
            base = base_ref[leaf]
            turned = mm(near_ref[leaf, 0], base).astype(BF)
            rotated = mm_t(base[:, :RANK], turned)
            corner = rotated[:, :RANK]
            matrix_ref[leaf] = 0.5 * (corner + corner.T)
            corner_ref[leaf] = rotated[:, RANK:].T

        sweep(matrix_ref, swept_ref, sweep_panel)
        for part in (0, 2, 1, 3):
            @pl.loop(0, SHARE, unroll=4)
            def _(owner):
                leaf = owner * SHARE + part
                gain_ref[part, owner] = (-mm_exact(corner_ref[leaf], matrix_ref[leaf])).astype(BF)

            pass_on(part)

    for copy in near_copies:
        copy.wait()

    @pl.loop(0, count, unroll=4)
    def _(leaf):
        base = base_ref[leaf]
        turned = [
            mm(near_ref[leaf, slot], wide_ref[place_ref[leaf, slot]]).astype(BF)
            for slot in range(2)
        ]
        rotated = mm_t(base, jnp.concatenate(turned, axis=1))
        right_ref[leaf] = rotated[:RANK].astype(BF)
        low_ref[leaf] = rotated[RANK:]

    def block_copy(part, off):
        owner = (mine + off) % SHARE
        return remote(packed_ref.at[part, owner], arrived_ref.at[part, mine], block_sems, (part, off - 1), at(line, owner))

    def take(part):
        gain_copy(part, (mine + 1) % SHARE).wait_recv()
        pass_on(part)

    def finish(part):
        @pl.loop(0, SHARE, unroll=4)
        def _(owner):
            leaf = owner * SHARE + part
            fix = mm(gain_ref[part, owner], right_ref[leaf])
            block = low_ref[leaf] - fix
            for slot in range(2):
                columns = slice(slot * RANK, (slot + 1) * RANK)
                skeleton_ref[leaf, slot] = block[:, columns]
                packed_ref[part, owner, slot] = block[:, columns].astype(BF)

        for off in range(1, SHARE):
            block_copy(part, off).start()
        arrived_ref[part, mine] = packed_ref[part, mine]

    shift = 2 * (mine // (SHARE - 1))
    parts = [(part + shift) % SHARE for part in range(SHARE)]

    @pl.when(mine != 0)
    def _():
        take(parts[0])
        take(parts[1])

    @pl.when(mine == 2)
    def _():
        take(parts[2])
        take(parts[3])

    finish(parts[0])
    finish(parts[1])

    @pl.when(mine % 2 == 1)
    def _():
        take(parts[2])

    finish(parts[2])

    @pl.when(mine % 2 == 1)
    def _():
        take(parts[3])

    finish(parts[3])
    for part in parts:
        for off in range(1, SHARE):
            block_copy(part, off).wait()
    for copy in upper_copies + label_copies:
        copy.wait()
    for part in range(SHARE):
        @pl.when((mine < SHARE - 1) if part < 2 else (mine != 1))
        def _():
            gain_copy(part, (mine + 1) % SHARE).wait_send()


def upper_kernel(label_ref, block_ref, base_ref, before_ref, after_ref, out_ref,
                 merged_ref, matrix_ref, swept_ref, right_ref, low_ref):
    parents = base_ref.shape[0]
    merged_ref[...] = jnp.zeros_like(merged_ref)
    for leaf in range(2 * parents):
        for slot in range(8):
            place = (leaf // 2) * 10 + label_ref[slot // 2, 2 * leaf + slot % 2, 0]
            rows = slice((leaf % 2) * RANK, (leaf % 2 + 1) * RANK)
            merged_ref[place, rows, :] = block_ref[leaf, slot // 2, slot % 2]
    for p in range(parents):
        base = base_ref[p]
        for d in range(5):
            left = jnp.concatenate([merged_ref[p * 10 + 2 * d], merged_ref[p * 10 + 2 * d + 1]], axis=1)
            q = p + d - 2
            if d == 2:
                partner = base
            elif q < 0:
                partner = before_ref[q + parents]
            elif q >= parents:
                partner = after_ref[q - parents]
            else:
                partner = base_ref[q, :, RANK:]
            mixed = mm(left, partner).astype(BF)
            lifted = mm_t(base, mixed)
            if d == 2:
                corner = lifted[:RANK, :RANK]
                matrix_ref[p] = 0.5 * (corner + corner.T)
                lifted = lifted[:, RANK:]
            right_ref[p, d] = lifted[:RANK]
            low_ref[p, d] = lifted[RANK:]
    sweep(matrix_ref, swept_ref, sweep_panel_by_four)
    for p in range(parents):
        gain = mm_exact(right_ref[p, 2].T, matrix_ref[p])
        for d in range(5):
            out_ref[p, d] = low_ref[p, d] + mm(gain.astype(BF), right_ref[p, d].astype(BF))


VM = pl.BlockSpec(memory_space=pltpu.VMEM)
SM = pl.BlockSpec(memory_space=pltpu.SMEM)
PARAMS = pltpu.CompilerParams(vmem_limit_bytes=48 * 1024 * 1024)


def shaped(shape, dtype):
    return jax.ShapeDtypeStruct(shape, dtype)


def exchange(place, label, near, base, upper_bases):
    count, parents = near.shape[0], upper_bases.shape[0]
    DMA = pltpu.SemaphoreType.DMA
    return pl.pallas_call(
        exchange_kernel,
        in_specs=[SM] + [VM] * 4,
        out_specs=[VM] * 5,
        out_shape=[
            shaped((count, 2, RANK, RANK), F32),
            shaped((SHARE, SHARE, 2, RANK, RANK), BF),
            shaped((SHARE, 8, RANK), jnp.int32),
            shaped((parents, BLK, RANK), BF),
            shaped((parents, BLK, RANK), BF),
        ],
        scratch_shapes=[
            pltpu.VMEM((count + 8, BLK, RANK), BF),
            pltpu.VMEM((SHARE, SHARE, RANK, RANK), BF),
            pltpu.VMEM((count, RANK, 2 * RANK), BF),
            pltpu.VMEM((count, RANK, 2 * RANK), F32),
            pltpu.VMEM((SHARE, SHARE, 2, RANK, RANK), BF),
            pltpu.VMEM((count, RANK, RANK), F32),
            pltpu.VMEM((count, RANK, RANK), F32),
            pltpu.VMEM((count, PANEL, RANK), F32),
            DMA((2, 2)), DMA((2, 2)), DMA((2, SHARE - 1)), DMA((2, SHARE)), DMA((2, SHARE, SHARE - 1)),
        ],
        compiler_params=pltpu.CompilerParams(
            vmem_limit_bytes=48 * 1024 * 1024, collective_id=0, has_side_effects=True
        ),
        name="exchange",
    )(place, label, near, base, upper_bases)


def upper(target, blocks, base, before, after):
    parents = base.shape[0]
    return pl.pallas_call(
        upper_kernel,
        in_specs=[SM] + [VM] * 4,
        out_specs=VM,
        out_shape=shaped((parents, 5, RANK, RANK), F32),
        scratch_shapes=[
            pltpu.VMEM((parents * 10, 2 * RANK, RANK), BF),
            pltpu.VMEM((parents, RANK, RANK), F32),
            pltpu.VMEM((parents, PANEL, RANK), F32),
            pltpu.VMEM((parents, 5, RANK, RANK), F32),
            pltpu.VMEM((parents, 5, RANK, RANK), F32),
        ],
        compiler_params=PARAMS,
        name="upper",
    )(target, blocks, base, before, after)


def per_device(near_blocks, leaf_bases, upper_bases, neighbours):
    count = near_blocks.shape[0]
    total = count * lax.axis_size(("node", "trow"))
    first_leaf = lax.axis_index(("node", "trow")) * count
    leaf_ids = first_leaf + jnp.arange(count, dtype=jnp.int32)
    target = 2 * ((neighbours // 2 - leaf_ids[:, None] // 2 + 2) % (total // 2)) + neighbours % 2
    label = jnp.broadcast_to(target.reshape(SHARE, 8, 1), (SHARE, 8, RANK))
    place = (neighbours - first_leaf + total // 2) % total - total // 2 + 4
    skeleton, arrived, labels, above, below = exchange(
        place, label, near_blocks, leaf_bases, upper_bases
    )
    upper_skeleton = upper(labels, arrived, upper_bases, above, below)
    return (skeleton, upper_skeleton)


def solution(mesh):
    return jax.shard_map(
        per_device,
        mesh=mesh,
        in_specs=(
            P(("node", "trow"), "tcol", None, None),
            P(("node", "trow"), None, None),
            P(("node", "trow", "tcol"), None, None),
            P(("node", "trow"), "tcol"),
        ),
        out_specs=(
            P(("node", "trow"), "tcol", None, None),
            P(("node", "trow", "tcol"), None, None, None),
        ),
        check_vma=False,
    )
```

time: 102 us -> 76.8 us (0.75)
  starting transfers between devices: 24.6 us -> 0 us
  waiting for transfers between devices: 13.6 us -> 0 us
  Pallas kernels: 57.4 us -> 70.3 us
  local copies, waits for them, and re-layouts: 3.51 us -> 4.85 us
    pallas_call x3 -> x1, Pallas kernels: 42.3 us -> 60.5 us  [exchange(): pl.pallas_call(exchange_kernel, in_specs=[SM] + [VM] * 4, out_specs=[VM]...]
    ppermute x7 -> x0, starting transfers between devices: 17.6 us -> none  [the longest x4 9.9 us: halo(): return (lax.ppermute(last, axis, up), lax.ppermute(initial, axis, down))]
    all_to_all x2 -> x0, waiting for transfers between devices: 12.4 us -> none  [the longest x1 12.4 us: per_device(): lax.all_to_all(packed, 'tcol', split_axis=0, concat_axis=1, tiled=True)]
    all_to_all x2 -> x0, starting transfers between devices: 7 us -> none  [the longest x1 3.77 us: per_device(): lax.all_to_all(packed, 'tcol', split_axis=0, concat_axis=1, tiled=True)]
    pallas_call x1, Pallas kernels: 15.1 us -> 9.81 us  [upper(): pl.pallas_call(upper_kernel, in_specs=[SM] + [VM] * 4, out_specs=VM, out_...]
    unnamed x7 -> x6, local copies, waits for them, and re-layouts: 1.68 us -> 4.61 us
    ppermute x7 -> x0, waiting for transfers between devices: 1.19 us -> none  [the longest x4 1.19 us: halo(): return (lax.ppermute(last, axis, up), lax.ppermute(initial, axis, down))]
    concatenate x1 -> x0, other arithmetic: 1.14 us -> none  [per_device(): wide = jnp.concatenate([before, skeleton_bases, after], axis=0)]
  transfers between devices with their start and end apart: 9 -> 0, of which waited for: 3 -> 0; matrix products, arithmetic and copies ran while one was open for 3% -> 0% of each run, Pallas kernels for 14% -> 0%
where the time goes in v2:
time: 76.8 us; the launch traced here: 76.6 us
  Pallas kernels  70.3 us (92%)
  local copies, waits for them, and re-layouts  4.85 us (6%)
  other arithmetic  0.79 us (1%)
    pallas_call x1, Pallas kernels, exchange(): pl.pallas_call(exchange_kernel, in_specs=[SM] + [VM] * 4, out_specs=[VM]...  60.5 us
    pallas_call x1, Pallas kernels, upper(): pl.pallas_call(upper_kernel, in_specs=[SM] + [VM] * 4, out_specs=VM, out_...  9.81 us
    unnamed x6, local copies, waits for them, and re-layouts  4.61 us

profile of v2, /device:TPU:96, one launch (start us, length us, event | category | flops | bytes accessed | tf_op | source)
XLA Modules:
  0.0 76.6 jit_solution(4623797429717451134)
XLA Ops:
  0.7 0.8 copy.19
  1.4 0.1 fusion.6
  1.5 0.1 broadcast_in_dim.8
  1.6 0.1 broadcast_in_dim.9.label_in_ref
  1.7 0.7 broadcast_subtract_fusion
  2.3 0.1 copy.18
  2.4 0.0 copy-start
  2.4 1.6 %copy-done = bf16[16,256,256]{2,1,0:T(8,128)(2,1)S(1)} copy-done((bf16[16,256,256]{2,1,0:T(8,128)(2,1)S(1)}, bf16[16,256,256]{2,1,0:T(8,128)(2,1)}, u32[]{:S(2)}) %copy-start) | copy-done | bytes 2097176
  4.0 0.0 copy-start.1
  4.0 0.9 %copy-done.1 = bf16[2,256,256]{2,1,0:T(8,128)(2,1)S(1)} copy-done((bf16[2,256,256]{2,1,0:T(8,128)(2,1)S(1)}, bf16[2,256,256]{2,1,0:T(8,128)(2,1)}, u32[]{:S(2)}) %copy-start.1) | copy-done | bytes 262168
  5.0 60.5 %exchange.1 = (f32[16,2,128,128]{3,2,1,0:T(8,128)S(1)}, bf16[4,4,2,128,128]{4,3,2,1,0:T(8,128)(2,1)S(1)}, s32[4,8,128]{2,1,0:T(8,128)S(1)}, bf16[2,256,128]{2,1,0:T(8,128)(2,1)S(1)}, bf16[2,256,128]{2,1,0:T(8,128)(2,1)S(1)}) custom-call(s32[16,2]{1,0:T(8,128)S(1)} %fusion.1.place_ref, s32[4,8,128]{2,1,0:T(8,128)S(1)} %broadcast_in_dim.9.label_in_ref, ...), custom_call_target="tpu_custom_call" | custom-call | tf_op jit(solution)/shard_map/exchange/pallas_call | solution.py:348
  65.5 9.8 %upper.1 = f32[2,5,128,128]{3,2,1,0:T(8,128)} custom-call(s32[4,8,128]{2,1,0:T(8,128)S(1)} %get-tuple-element.8.label_ref, bf16[4,4,2,128,128]{4,3,2,1,0:T(8,128)(2,1)S(1)} %get-tuple-element.9.block_ref, bf16[2,256,256]{2,1,0:T(8,128)(2,1)S(1)} %copy-done.1, bf16[2,256,128]{2,1,0:T(8,128)(2,1)S(1)} %get-tuple-element.10.before_ref, ...), custom_call_target="tpu_custom_call" | custom-call | tf_op jit(solution)/shard_map/upper/pallas_call | solution.py:379
  75.3 1.3 %copy.24 = f32[16,2,128,128]{3,2,1,0:T(8,128)} copy(f32[16,2,128,128]{3,2,1,0:T(8,128)S(1)} %get-tuple-element.14) | data formatting | bytes 4194304
  (2 shorter events, 0.0 us)
Async XLA Ops:
  2.4 1.6 %copy-start = (bf16[16,256,256]{2,1,0:T(8,128)(2,1)S(1)}, bf16[16,256,256]{2,1,0:T(8,128)(2,1)}, u32[]{:S(2)}) copy-start(bf16[16,256,256]{2,1,0:T(8,128)(2,1)} %base_ref.2) | copy-start | bytes 6291460
  4.0 0.9 %copy-start.1 = (bf16[2,256,256]{2,1,0:T(8,128)(2,1)S(1)}, bf16[2,256,256]{2,1,0:T(8,128)(2,1)}, u32[]{:S(2)}) copy-start(bf16[2,256,256]{2,1,0:T(8,128)(2,1)} %base_ref.3) | copy-start | bytes 786436
